TPU v7x, 256 devices: a whole 4x4x8 slice. The times are simulated.
256 devices in a mesh: tok: 32 (over x, y, core), feat: 8 (over z).
Axes of the slice: x: 4, y: 4, z: 8, core: 2. Of those that a mesh axis runs over, the one named last changes fastest.
Arguments:
- inputs: bfloat16 [16384, 2048], P(('tok', 'feat'))
- norm_gain: float32 [2048], replicated, may hold values from 0.1 to 1.9
- w_in: bfloat16 [512, 8192], P('tok', 'feat'), may hold values from -0.25 to 0.25
- w_out: bfloat16 [512, 8192], P('tok', 'feat'), may hold values from -0.125 to 0.125
- block_index: int32 [64, 4], P('feat'), may hold values from 0 to 15, all different within a row
- segment_ids: int32 [16384], P(('tok', 'feat')), may hold values from 0 to 1023, never falling along the last dimension, each value on 1 to 24 neighbouring positions
- teacher_scores: float32 [1024], replicated, may hold values from -6 to 6
- upstream: bfloat16 [16384, 2048], P(('tok', 'feat')), may hold values from -6 to 6
- readout: float32 [2048], replicated, may hold values from -0.125 to 0.125
Outputs:
- layer_out: bfloat16 [16384, 2048], P(('tok', 'feat'))
- input_grad: bfloat16 [16384, 2048], P(('tok', 'feat'))
- grad_in: float32 [512, 8192], P('tok', 'feat')
- grad_out: float32 [512, 8192], P('tok', 'feat')
Inputs may be any that keep to these rules, and one draw needn't show every extreme that they name: `block_index`: each row names 4 different feature blocks; every feature block is named by some row. `segment_ids`: never falls along the tokens; every segment 0 to 1023 holds 1 to 24 tokens.
All inputs are finite; a program needn't handle non-finite values.
Results may differ from a plain program's by a relative error of at most 0.015.
Values may be sent and summed in bfloat16 or wider, within the bound.
A program may use at most 128 MiB of HBM per device.

v0:
```python
import math
import jax
import jax.numpy as jnp
from jax import lax
from jax.sharding import PartitionSpec as P

BLK = 128
EPS = 1e-06
LOSS_WEIGHT = 8.0


def gelu_tanh(values):
    return jax.nn.gelu(values, approximate=True)


def gelu_back(values, cotangent):
    return jax.vjp(gelu_tanh, values)[1](cotangent)[0]


def on_device(
    inputs, norm_gain, w_in, w_out, block_index, segment_ids, teacher_scores, upstream, readout
):
    local_tokens, model_width = inputs.shape
    blocks_here = w_in.shape[1] // BLK
    feature_blocks = model_width // BLK
    per_hidden = block_index.shape[1]
    total_tokens = local_tokens * lax.axis_size("tok") * lax.axis_size("feat")
    grad_scale = 1.0 / math.sqrt(total_tokens)
    inputs_wide = inputs.astype(jnp.float32)
    mean_square = jnp.mean(inputs_wide * inputs_wide, axis=1, keepdims=True)
    inv_rms = lax.rsqrt(mean_square + EPS)
    normed = (inputs_wide * inv_rms * norm_gain[None, :]).astype(jnp.bfloat16)
    w_in_all, w_out_all = (
        lax.all_gather(w_in, "tok", axis=0, tiled=True),
        lax.all_gather(w_out, "tok", axis=0, tiled=True),
    )
    picked_width = w_in_all.shape[0]
    w_in_blocks = w_in_all.reshape(picked_width, blocks_here, BLK)
    w_out_blocks = w_out_all.reshape(picked_width, blocks_here, BLK)
    normed_rows = lax.all_gather(normed, "feat", axis=0, tiled=True)
    group_rows = normed_rows.shape[0]
    one_hot = block_index[:, :, None] == jnp.arange(feature_blocks, dtype=jnp.int32)[None, None, :]
    sel_half = one_hot.astype(jnp.bfloat16)
    sel_wide = one_hot.astype(jnp.float32)

    def select(rows):
        blocks = rows.reshape(group_rows, feature_blocks, BLK)
        picked = jnp.einsum("rdc,jkd->rjkc", blocks, sel_half, preferred_element_type=jnp.float32)
        return picked.astype(jnp.bfloat16).reshape(group_rows, blocks_here, picked_width)

    def spread(terms):
        grouped = terms.reshape(group_rows, blocks_here, per_hidden, BLK)
        placed = jnp.einsum("rjkc,jkd->rdc", grouped, sel_wide, precision=lax.Precision.HIGHEST)
        return placed.reshape(group_rows, model_width)

    chosen = select(normed_rows)
    pre_act = jnp.einsum("rjm,mjc->rjc", chosen, w_in_blocks, preferred_element_type=jnp.float32)
    activated = gelu_tanh(pre_act).astype(jnp.bfloat16)
    out_terms_fwd = jnp.einsum(
        "rjc,mjc->rjm", activated, w_out_blocks, preferred_element_type=jnp.float32
    )
    branch = lax.psum_scatter(
        spread(out_terms_fwd).astype(jnp.bfloat16), "feat", scatter_dimension=0, tiled=True
    ).astype(jnp.float32)
    layer_out = (inputs_wide + branch).astype(jnp.bfloat16)
    token_score = jnp.dot(layer_out.astype(jnp.float32), readout, precision=lax.Precision.HIGHEST)
    segment_count = teacher_scores.shape[0]
    member = (segment_ids[:, None] == jnp.arange(segment_count, dtype=jnp.int32)[None, :]).astype(
        jnp.float32
    )
    score_sums = jnp.dot(token_score, member, precision=lax.Precision.HIGHEST)
    token_counts = jnp.sum(member, axis=0)
    score_sums, token_counts = lax.psum((score_sums, token_counts), ("tok", "feat"))
    misfit = score_sums / token_counts - teacher_scores
    token_coeff = 2.0 * LOSS_WEIGHT * jnp.sum(member * misfit[None, :], axis=1)
    cotangent_local = (
        upstream.astype(jnp.float32) + token_coeff[:, None] * readout[None, :]
    ).astype(jnp.bfloat16)
    cotangent_rows = lax.all_gather(cotangent_local, "feat", axis=0, tiled=True)
    chosen_grad = select(cotangent_rows)
    upper_grad = jnp.einsum(
        "rjm,mjc->rjc", chosen_grad, w_out_blocks, preferred_element_type=jnp.float32
    )
    pre_grad = gelu_back(pre_act, upper_grad).astype(jnp.bfloat16)

    def arrange(terms):
        return terms.reshape(picked_width, blocks_here * BLK) * grad_scale

    back_terms = jnp.einsum(
        "rjc,mjc->rjm", pre_grad, w_in_blocks, preferred_element_type=jnp.float32
    )
    out_terms = jnp.einsum(
        "rjm,rjc->mjc", chosen_grad, activated, preferred_element_type=jnp.float32
    )
    in_terms = jnp.einsum("rjm,rjc->mjc", chosen, pre_grad, preferred_element_type=jnp.float32)
    grad_out, grad_in = (
        lax.psum_scatter(
            arrange(out_terms).astype(jnp.bfloat16), "tok", scatter_dimension=0, tiled=True
        ).astype(jnp.float32),
        lax.psum_scatter(
            arrange(in_terms).astype(jnp.bfloat16), "tok", scatter_dimension=0, tiled=True
        ).astype(jnp.float32),
    )
    back_sum = lax.psum_scatter(
        spread(back_terms).astype(jnp.bfloat16), "feat", scatter_dimension=0, tiled=True
    ).astype(jnp.float32)
    scaled = back_sum * norm_gain[None, :]
    inner_mean = jnp.mean(scaled * inputs_wide, axis=1, keepdims=True)
    norm_back = inv_rms * scaled - inputs_wide * (inv_rms * inv_rms * inv_rms) * inner_mean
    input_grad = (cotangent_local.astype(jnp.float32) + norm_back).astype(jnp.bfloat16)
    return (layer_out, input_grad, grad_in, grad_out)


def solution(mesh):
    return jax.shard_map(
        on_device,
        mesh=mesh,
        in_specs=(
            P(("tok", "feat"), None),
            P(),
            P("tok", "feat"),
            P("tok", "feat"),
            P("feat", None),
            P(("tok", "feat")),
            P(),
            P(("tok", "feat"), None),
            P(),
        ),
        out_specs=(
            P(("tok", "feat"), None),
            P(("tok", "feat"), None),
            P("tok", "feat"),
            P("tok", "feat"),
        ),
        check_vma=False,
    )
```

profile of v0, /device:TPU:2, one launch (start us, length us, event | category | flops | bytes accessed | tf_op | source)
XLA Modules:
  0.0 581.6 jit_solution(5638336384249948303)
XLA Ops:
  7.2 0.0 all-gather.7.cloned.1.call-start
  7.2 0.7 all-gather.7.cloned.1.call-update
  7.9 0.0 all-gather.9.cloned.1.call-start
  7.9 0.7 all-gather.9.cloned.1.call-update
  8.6 0.0 all-gather.5.cloned.1.call-start
  8.7 1.1 fusion.25
  9.8 1.8 fusion.27
  11.6 0.0 all-gather.5.cloned.1.call-update
  11.6 0.0 reduce-scatter.5.cloned.1.call-start
  11.7 49.1 %all-gather.7.cloned.1.call-done = bf16[512,1024]{1,0:T(8,128)(2,1)} async-done(((bf16[16,1024]{1,0:T(8,128)(2,1)}), bf16[512,1024]{1,0:T(8,128)(2,1)}) %all-gather.7.cloned.1.call-update) | async-done | bytes 1048592 | tf_op jit(solution)/shard_map/all_gather | solution.py:34
  60.8 1.5 copy.56
  62.3 48.1 %all-gather.9.cloned.1.call-done = bf16[512,1024]{1,0:T(8,128)(2,1)} async-done(((bf16[16,1024]{1,0:T(8,128)(2,1)}), bf16[512,1024]{1,0:T(8,128)(2,1)}) %all-gather.9.cloned.1.call-update) | async-done | bytes 1048592 | tf_op jit(solution)/shard_map/all_gather | solution.py:35
  110.3 1.5 copy.59
  111.8 41.5 %all-gather.5.cloned.1.call-done = bf16[512,2048]{1,0:T(8,128)(2,1)} async-done(((bf16[64,2048]{1,0:T(8,128)(2,1)}), bf16[512,2048]{1,0:T(8,128)(2,1)}) %all-gather.5.cloned.1.call-update) | async-done | bytes 2097168 | tf_op jit(solution)/shard_map/all_gather | solution.py:40
  153.3 2.2 copy.82
  155.5 1.3 convert_bitcast_fusion.1
  156.8 0.7 copy.105
  157.6 1.4 fusion.6
  159.0 0.6 copy-done.1
  159.5 4.5 fusion.47
  164.1 10.4 %copy.61 = f32[512,8,4,128]{3,1,2,0:T(8,128)} copy(f32[512,8,4,128]{0,3,2,1:T(8,128)} %bitcast.104) | data formatting | bytes 16777216 | tf_op jit(solution)/shard_map/reshape | solution.py:52
  174.5 5.6 bitcast_convert_fusion.1
  180.1 1.9 copy.107
  182.0 0.0 reduce-scatter.5.cloned.1.call-update
  182.0 0.0 all-gather.11.cloned.1.call-start
  182.1 0.6 copy-done.16
  182.6 0.1 convert_reduce_fusion
  182.7 40.9 %reduce-scatter.5.cloned.1.call-done = bf16[64,2048]{1,0:T(8,128)(2,1)} async-done(((bf16[512,2048]{1,0:T(8,128)(2,1)}), bf16[64,2048]{1,0:T(8,128)(2,1)}) %reduce-scatter.5.cloned.1.call-update) | async-done | bytes 262160 | tf_op jit(solution)/shard_map/reduce_scatter | solution.py:62
  223.6 1.0 fusion.28
  224.6 0.0 copy-start.11
  224.6 0.7 copy-done.11
  225.3 0.3 convolution_bitcast_fusion
  225.6 0.3 fusion.34
  225.9 74.4 %all-reduce = (f32[1024]{0:T(1024)S(1)}, f32[1024]{0:T(1024)S(1)}) all-reduce(f32[1024]{0:T(1024)S(1)} %bitcast.124, f32[1024]{0:T(1024)S(1)} %convert_reduce_fusion), channel_id=1, replica_groups=mesh['tok'=32,'feat'=8] {'tok','feat'}, use_global_device_ids=true, to_apply=%region_2.0 | all-reduce | flops 2048 | bytes 16384 | tf_op jit(solution)/shard_map/psum | solution.py:73
  300.3 0.2 select_reduce_fusion
  300.5 0.8 add_convert_fusion
  301.4 0.0 all-gather.11.cloned.1.call-update
  301.4 0.2 reduce-scatter.9.cloned.1.call-start
  301.6 37.5 %all-gather.11.cloned.1.call-done = bf16[512,2048]{1,0:T(8,128)(2,1)} async-done(((bf16[64,2048]{1,0:T(8,128)(2,1)}), bf16[512,2048]{1,0:T(8,128)(2,1)}) %all-gather.11.cloned.1.call-update) | async-done | bytes 2097168 | tf_op jit(solution)/shard_map/all_gather | solution.py:79
  339.1 2.2 copy.84
  341.3 1.3 convert_bitcast_fusion
  342.6 0.7 copy.104
  343.3 0.8 copy-done.5
  344.2 3.7 fusion.14
  347.9 3.6 multiply_convert_fusion.1
  351.5 2.4 copy.69
  353.9 0.0 reduce-scatter.9.cloned.1.call-update
  353.9 0.0 reduce-scatter.11.cloned.1.call-start
  354.0 6.2 %multiply_convert_fusion = bf16[8,128,512]{2,1,0:T(8,128)(2,1)} fusion(bf16[512,8,512]{2,1,0:T(8,128)(2,1)} %bitcast.116, f32[8,512,128]{2,1,0:T(8,128)S(1)} %copy-done.6), kind=kOutput, calls=%fused_computation.32 | convolution fusion | flops 542638080 | bytes 7340032 | tf_op jit(solution)/shard_map/rjm,rjc->mjc/dot_general | solution.py:92
  360.2 2.4 copy.72
  362.5 0.0 reduce-scatter.11.cloned.1.call-update
  362.6 0.3 reduce-scatter.7.cloned.1.call-start
  362.8 4.5 fusion.49
  367.4 10.5 %copy.66 = f32[512,8,4,128]{3,1,2,0:T(8,128)} copy(f32[512,8,4,128]{0,3,2,1:T(8,128)} %bitcast.103) | data formatting | bytes 16777216 | tf_op jit(solution)/shard_map/reshape | solution.py:52
  377.8 5.6 bitcast_convert_fusion
  383.5 1.9 copy.106
  385.4 0.0 reduce-scatter.7.cloned.1.call-update
  385.4 52.5 %reduce-scatter.9.cloned.1.call-done = bf16[16,1024]{1,0:T(8,128)(2,1)} async-done(((bf16[512,1024]{1,0:T(8,128)(2,1)}), bf16[16,1024]{1,0:T(8,128)(2,1)}) %reduce-scatter.9.cloned.1.call-update) | async-done | bytes 32784 | tf_op jit(solution)/shard_map/reduce_scatter | solution.py:100
  437.8 1.4 convert_element_type.118
  439.2 87.3 %reduce-scatter.11.cloned.1.call-done = bf16[16,1024]{1,0:T(8,128)(2,1)} async-done(((bf16[512,1024]{1,0:T(8,128)(2,1)}), bf16[16,1024]{1,0:T(8,128)(2,1)}) %reduce-scatter.11.cloned.1.call-update) | async-done | bytes 32784 | tf_op jit(solution)/shard_map/reduce_scatter | solution.py:97
  526.5 1.4 convert_element_type.122
  527.9 43.7 %reduce-scatter.7.cloned.1.call-done = bf16[64,2048]{1,0:T(8,128)(2,1)} async-done(((bf16[512,2048]{1,0:T(8,128)(2,1)}), bf16[64,2048]{1,0:T(8,128)(2,1)}) %reduce-scatter.7.cloned.1.call-update) | async-done | bytes 262160 | tf_op jit(solution)/shard_map/reduce_scatter | solution.py:104
  571.6 1.1 fusion.33
  572.8 2.0 fusion.32
  (33 shorter events, 0.1 us)
Async XLA Ops:
  7.2 53.6 %all-gather.7.cloned.1.call-start = ((), (), s32[]{:S(2)}) async-start(), calls=%async_computation.5 | async-start | bytes 1081344 | tf_op jit(solution)/shard_map/all_gather | solution.py:34
  7.9 102.4 %all-gather.9.cloned.1.call-start = ((), (), s32[]{:S(2)}) async-start(), calls=%async_computation.6 | async-start | bytes 1081344 | tf_op jit(solution)/shard_map/all_gather | solution.py:35
  8.6 144.7 %all-gather.5.cloned.1.call-start = ((), (), s32[]{:S(2)}) async-start(), calls=%async_computation.4 | async-start | bytes 2359296 | tf_op jit(solution)/shard_map/all_gather | solution.py:40
  11.6 212.0 %reduce-scatter.5.cloned.1.call-start = ((), (), s32[]{:S(2)}) async-start(), calls=%async_computation.7 | async-start | bytes 2359296 | tf_op jit(solution)/shard_map/reduce_scatter | solution.py:62
  153.3 2.2 copy-start.12
  157.6 2.0 copy-start.1
  159.5 4.6 copy-start.4
  182.0 0.7 copy-start.16
  182.0 41.6 %copy-start = (bf16[64,2048]{1,0:T(8,128)(2,1)S(1)}, bf16[64,2048]{1,0:T(8,128)(2,1)}, u32[]{:S(2)}) copy-start(bf16[64,2048]{1,0:T(8,128)(2,1)} %param.9) | copy-start | bytes 786436
  182.0 43.4 %copy-start.14 = (f32[2048]{0:T(1024)S(1)}, f32[2048]{0:T(1024)}, u32[]{:S(2)}) copy-start(f32[2048]{0:T(1024)} %param.17) | copy-start | bytes 24580
  182.0 118.3 %copy-start.15 = (f32[1024]{0:T(1024)S(1)}, f32[1024]{0:T(1024)}, u32[]{:S(2)}) copy-start(f32[1024]{0:T(1024)} %param.15) | copy-start | bytes 12292
  182.0 118.5 %copy-start.9 = (bf16[64,2048]{1,0:T(8,128)(2,1)S(1)}, bf16[64,2048]{1,0:T(8,128)(2,1)}, u32[]{:S(2)}) copy-start(bf16[64,2048]{1,0:T(8,128)(2,1)} %param.16) | copy-start | bytes 786436
  182.0 157.0 %all-gather.11.cloned.1.call-start = ((), (), s32[]{:S(2)}) async-start(), calls=%async_computation.8 | async-start | bytes 2359296 | tf_op jit(solution)/shard_map/all_gather | solution.py:79
  224.6 0.7 copy-start.11
  301.4 136.4 %reduce-scatter.9.cloned.1.call-start = ((), (), s32[]{:S(2)}) async-start(), calls=%async_computation.10 | async-start | bytes 1081344 | tf_op jit(solution)/shard_map/reduce_scatter | solution.py:100
  342.6 1.6 copy-start.5
  343.3 4.5 copy-start.3
  344.2 3.7 copy-start.2
  347.9 3.6 copy-start.7
  351.5 2.5 copy-start.6
  353.9 172.6 %reduce-scatter.11.cloned.1.call-start = ((), (), s32[]{:S(2)}) async-start(), calls=%async_computation.11 | async-start | bytes 1081344 | tf_op jit(solution)/shard_map/reduce_scatter | solution.py:97
  360.2 2.7 copy-start.8
  362.6 209.1 %reduce-scatter.7.cloned.1.call-start = ((), (), s32[]{:S(2)}) async-start(), calls=%async_computation.9 | async-start | bytes 2359296 | tf_op jit(solution)/shard_map/reduce_scatter | solution.py:104
  385.3 186.3 %copy-start.13 = (f32[2048]{0:T(1024)S(1)}, f32[2048]{0:T(1024)}, u32[]{:S(2)}) copy-start(f32[2048]{0:T(1024)} %param.10) | copy-start | bytes 24580
  385.4 187.4 %copy-start.10 = (bf16[64,2048]{1,0:T(8,128)(2,1)S(1)}, bf16[64,2048]{1,0:T(8,128)(2,1)}, u32[]{:S(2)}) copy-start(bf16[64,2048]{1,0:T(8,128)(2,1)} %param.16) | copy-start | bytes 786436
Sparse Core Ops, SparseCore 0:
  10.5 50.1 all-gather.6
  63.3 46.9 all-gather.8
  112.7 40.5 all-gather.4
  182.1 41.4 reduce-scatter.4
  301.5 37.5 all-gather.10
  354.1 83.7 reduce-scatter.8
  441.6 84.8 reduce-scatter.10
  529.1 42.5 reduce-scatter.6
where the time goes:
time: 583 us; the launch traced here: 582 us
  waiting for transfers between devices  402 us (69%)
  blocking collectives  74.4 us (13%)
  local copies, waits for them, and re-layouts  41 us (7%)
  matrix products  38.3 us (7%)
  between operations  14.4 us (2%)
  other arithmetic  11 us (2%)
    reduce_scatter x1, waiting for transfers between devices, on_device(): lax.psum_scatter(arrange(out_terms).astype(jnp.bfloat16), 'tok', scatter_...  87.3 us
    psum x1, blocking collectives, on_device(): lax.psum((score_sums, token_counts), ('tok', 'feat'))  74.4 us
    reduce_scatter x1, waiting for transfers between devices, on_device(): lax.psum_scatter(arrange(in_terms).astype(jnp.bfloat16), 'tok', scatter_d...  52.5 us
    all_gather x1, waiting for transfers between devices, on_device(): lax.all_gather(w_in, 'tok', axis=0, tiled=True)  49.1 us
    all_gather x1, waiting for transfers between devices, on_device(): lax.all_gather(w_out, 'tok', axis=0, tiled=True)  48.1 us
    reduce_scatter x1, waiting for transfers between devices, on_device(): lax.psum_scatter(spread(back_terms).astype(jnp.bfloat16), 'feat', scatter...  43.7 us
    all_gather x1, waiting for transfers between devices, on_device(): normed_rows = lax.all_gather(normed, 'feat', axis=0, tiled=True)  41.5 us
    reduce_scatter x1, waiting for transfers between devices, on_device(): lax.psum_scatter(spread(out_terms_fwd).astype(jnp.bfloat16), 'feat', scat...  40.9 us
  transfers between devices with their start and end apart: 8, of which 8 were waited for; matrix products, arithmetic and copies ran while one was open for 7% of the time, Pallas kernels for 0%

commit v1 on v0

--- a/solution.py
+++ b/solution.py
@@ -37,7 +37,16 @@
     picked_width = w_in_all.shape[0]
     w_in_blocks = w_in_all.reshape(picked_width, blocks_here, BLK)
     w_out_blocks = w_out_all.reshape(picked_width, blocks_here, BLK)
-    normed_rows = lax.all_gather(normed, "feat", axis=0, tiled=True)
+    ways = lax.axis_size("feat")
+    up = [(d, (d + 1) % ways) for d in range(ways)]
+    down = [(d, (d - 1) % ways) for d in range(ways)]
+    earlier, later = ([normed], [normed])
+    for _ in range(ways // 2):
+        earlier.append(lax.ppermute(earlier[-1], "feat", up))
+    for _ in range((ways - 1) // 2):
+        later.append(lax.ppermute(later[-1], "feat", down))
+    line = jnp.concatenate([*earlier[::-1], *later[1:]], axis=0)
+    normed_rows = jnp.roll(line, (lax.axis_index("feat") - ways // 2) * normed.shape[0], axis=0)
     group_rows = normed_rows.shape[0]
     one_hot = block_index[:, :, None] == jnp.arange(feature_blocks, dtype=jnp.int32)[None, None, :]
     sel_half = one_hot.astype(jnp.bfloat16)

time: 583 us -> 532 us (0.913)
  waiting for transfers between devices: 402 us -> 338 us
  starting transfers between devices: 0.72 us -> 12.7 us
    all_gather x1 -> x0, waiting for transfers between devices: 41.5 us -> none  [on_device(): normed_rows = lax.all_gather(normed, 'feat', axis=0, tiled=True)]
    all_gather x1, waiting for transfers between devices: 49.1 us -> 7.75 us  [on_device(): lax.all_gather(w_in, 'tok', axis=0, tiled=True)]
    reduce_scatter x1, waiting for transfers between devices: 87.3 us -> 51.3 us  [on_device(): lax.psum_scatter(arrange(out_terms).astype(jnp.bfloat16), 'tok', scatter_...]
    reduce_scatter x1, waiting for transfers between devices: 52.5 us -> 87.2 us  [on_device(): lax.psum_scatter(arrange(in_terms).astype(jnp.bfloat16), 'tok', scatter_d...]
    ppermute x0 -> x7, waiting for transfers between devices: none -> 24.3 us  [the longest x4 24.3 us: on_device(): earlier.append(lax.ppermute(earlier[-1], 'feat', up))]
    ppermute x0 -> x7, starting transfers between devices: none -> 12 us  [the longest x3 9.96 us: on_device(): later.append(lax.ppermute(later[-1], 'feat', down))]
  transfers between devices with their start and end apart: 8 -> 14, of which waited for: 8 -> 11; matrix products, arithmetic and copies ran while one was open for 7% -> 9% of each run, Pallas kernels for 0% -> 0%
where the time goes in v1:
time: 532 us; the launch traced here: 531 us
  waiting for transfers between devices  338 us (64%)
  blocking collectives  74.4 us (14%)
  matrix products  41.3 us (8%)
  local copies, waits for them, and re-layouts  38.6 us (7%)
  between operations  14.6 us (3%)
  starting transfers between devices  12.7 us (2%)
  other arithmetic  11.5 us (2%)
    reduce_scatter x1, waiting for transfers between devices, on_device(): lax.psum_scatter(arrange(in_terms).astype(jnp.bfloat16), 'tok', scatter_d...  87.2 us
    psum x1, blocking collectives, on_device(): lax.psum((score_sums, token_counts), ('tok', 'feat'))  74.4 us
    reduce_scatter x1, waiting for transfers between devices, on_device(): lax.psum_scatter(arrange(out_terms).astype(jnp.bfloat16), 'tok', scatter_...  51.3 us
    reduce_scatter x1, waiting for transfers between devices, on_device(): lax.psum_scatter(spread(back_terms).astype(jnp.bfloat16), 'feat', scatter...  43.8 us
    all_gather x1, waiting for transfers between devices, on_device(): lax.all_gather(w_out, 'tok', axis=0, tiled=True)  43.1 us
    reduce_scatter x1, waiting for transfers between devices, on_device(): lax.psum_scatter(spread(out_terms_fwd).astype(jnp.bfloat16), 'feat', scat...  42.5 us
    all_gather x1, waiting for transfers between devices, on_device(): cotangent_rows = lax.all_gather(cotangent_local, 'feat', axis=0, tiled=True)  37.4 us
    ppermute x4, waiting for transfers between devices, on_device(): earlier.append(lax.ppermute(earlier[-1], 'feat', up))  24.3 us
  transfers between devices with their start and end apart: 14, of which 11 were waited for; matrix products, arithmetic and copies ran while one was open for 9% of the time, Pallas kernels for 0%

profile of v1, /device:TPU:2, one launch (start us, length us, event | category | flops | bytes accessed | tf_op | source)
XLA Modules:
  0.0 531.2 jit_solution(3993007331588601763)
XLA Ops:
  7.2 0.0 all-gather.4.cloned.1.call-start
  7.2 0.7 all-gather.4.cloned.1.call-update
  7.9 0.0 all-gather.6.cloned.1.call-start
  8.0 1.1 fusion.25
  9.1 1.1 fusion.27
  10.2 2.0 collective-permute-start
  12.2 10.2 %collective-permute-done = bf16[64,2048]{1,0:T(8,128)(2,1)S(1)} collective-permute-done((bf16[64,2048]{1,0:T(8,128)(2,1)S(1)}, bf16[64,2048]{1,0:T(8,128)(2,1)S(1)}, u32[]{:S(2)}, u32[]{:S(2)}) %collective-permute-start) | collective-permute-done | bytes 262176 | tf_op jit(solution)/shard_map/ppermute | solution.py:45
  22.4 3.2 collective-permute-start.4
  25.7 5.4 %collective-permute-done.1 = bf16[64,2048]{1,0:T(8,128)(2,1)S(1)} collective-permute-done((bf16[64,2048]{1,0:T(8,128)(2,1)S(1)}, bf16[64,2048]{1,0:T(8,128)(2,1)S(1)}, u32[]{:S(2)}, u32[]{:S(2)}) %collective-permute-start.1) | collective-permute-done | bytes 262176 | tf_op jit(solution)/shard_map/ppermute | solution.py:45
  31.1 3.2 collective-permute-start.5
  34.3 4.6 collective-permute-done.2
  38.9 0.0 all-gather.6.cloned.1.call-update
  39.0 0.0 reduce-scatter.5.cloned.1.call-start
  39.0 3.5 collective-permute-start.6
  42.5 4.0 collective-permute-done.3
  46.6 1.1 constant_dynamic-update-slice_fusion.11
  47.9 0.1 constant_dynamic-update-slice_fusion.3
  48.2 0.2 dynamic-slice_bitcast_fusion
  48.4 0.6 copy.82
  49.1 1.3 convert_bitcast_fusion.1
  50.4 2.7 copy.105
  53.0 7.8 %all-gather.4.cloned.1.call-done = bf16[512,1024]{1,0:T(8,128)(2,1)} async-done(((bf16[16,1024]{1,0:T(8,128)(2,1)}), bf16[512,1024]{1,0:T(8,128)(2,1)}) %all-gather.4.cloned.1.call-update) | async-done | bytes 1048592 | tf_op jit(solution)/shard_map/all_gather | solution.py:34
  60.8 1.5 copy.56
  62.3 4.9 fusion.6
  67.2 43.1 %all-gather.6.cloned.1.call-done = bf16[512,1024]{1,0:T(8,128)(2,1)} async-done(((bf16[16,1024]{1,0:T(8,128)(2,1)}), bf16[512,1024]{1,0:T(8,128)(2,1)}) %all-gather.6.cloned.1.call-update) | async-done | bytes 1048592 | tf_op jit(solution)/shard_map/all_gather | solution.py:35
  110.3 1.5 copy.59
  111.8 6.1 %fusion.47 = f32[8,512,512]{1,2,0:T(8,128)} fusion(bf16[512,8,128]{0,2,1:T(8,128)(2,1)S(1)} %bitcast.118, f32[8,512,128]{2,1,0:T(8,128)} %fusion.6), kind=kOutput, calls=%fused_computation.85 | convolution fusion | flops 541589504 | bytes 11534336 | tf_op jit(solution)/shard_map/rjc,mjc->rjm/dot_general | solution.py:68
  118.0 10.4 %copy.61 = f32[512,8,4,128]{3,1,2,0:T(8,128)} copy(f32[512,8,4,128]{0,3,2,1:T(8,128)} %bitcast.105) | data formatting | bytes 16777216 | tf_op jit(solution)/shard_map/reshape | solution.py:61
  128.4 5.6 %bitcast_convert_fusion.1 = bf16[16,512,128]{2,0,1:T(8,128)(2,1)S(1)} fusion(f32[512,8,4,128]{3,1,2,0:T(8,128)} %copy.61, s32[8,4]{0,1:T(4,128)S(1)} %copy-done.8), kind=kOutput, calls=%fused_computation.1 | convolution fusion | flops 403702272 | bytes 10485888 | tf_op jit(solution)/shard_map/rjkc,jkd->rdc/dot_general | solution.py:62
  134.1 1.9 copy.107
  136.0 0.0 all-gather.8.cloned.1.call-start
  136.0 0.1 convert_reduce_fusion
  136.1 42.5 %reduce-scatter.5.cloned.1.call-done = bf16[64,2048]{1,0:T(8,128)(2,1)} async-done(((bf16[512,2048]{1,0:T(8,128)(2,1)}), bf16[64,2048]{1,0:T(8,128)(2,1)}) %reduce-scatter.5.cloned.1.call-update) | async-done | bytes 262160 | tf_op jit(solution)/shard_map/reduce_scatter | solution.py:71
  178.6 1.0 fusion.28
  179.7 0.7 copy-done.6
  180.4 0.3 convolution_bitcast_fusion
  180.7 0.3 fusion.34
  180.9 74.4 %all-reduce = (f32[1024]{0:T(1024)S(1)}, f32[1024]{0:T(1024)S(1)}) all-reduce(f32[1024]{0:T(1024)S(1)} %bitcast.124, f32[1024]{0:T(1024)S(1)} %convert_reduce_fusion), channel_id=1, replica_groups=mesh['tok'=32,'feat'=8] {'tok','feat'}, use_global_device_ids=true, to_apply=%region_2.3 | all-reduce | flops 2048 | bytes 16384 | tf_op jit(solution)/shard_map/psum | solution.py:82
  255.4 0.2 select_reduce_fusion
  255.6 0.8 add_convert_fusion
  256.5 0.3 reduce-scatter.11.cloned.1.call-start
  256.7 37.4 %all-gather.8.cloned.1.call-done = bf16[512,2048]{1,0:T(8,128)(2,1)} async-done(((bf16[64,2048]{1,0:T(8,128)(2,1)}), bf16[512,2048]{1,0:T(8,128)(2,1)}) %all-gather.8.cloned.1.call-update) | async-done | bytes 2097168 | tf_op jit(solution)/shard_map/all_gather | solution.py:88
  294.2 2.2 copy.84
  296.4 1.3 convert_bitcast_fusion
  297.7 0.7 copy.104
  298.4 0.8 copy-done.3
  299.2 3.0 multiply_convert_fusion
  302.3 1.3 copy.72
  303.6 0.0 reduce-scatter.9.cloned.1.call-start
  303.7 5.6 %fusion.14 = bf16[512,8,128]{2,0,1:T(8,128)(2,1)S(1)} fusion(f32[8,512,128]{2,1,0:T(8,128)} %fusion.6, bf16[512,8,128]{0,2,1:T(8,128)(2,1)S(1)} %bitcast.119, bf16[512,8,512]{2,1,0:T(8,128)(2,1)} %bitcast.117), kind=kOutput, calls=%fused_computation.22 | convolution fusion | flops 547356672 | bytes 8388608 | tf_op jit(solution)/shard_map/rjm,mjc->rjc/dot_general | solution.py:90
  309.3 2.8 multiply_convert_fusion.1
  312.0 1.3 copy.69
  313.4 0.3 reduce-scatter.7.cloned.1.call-start
  313.7 4.5 fusion.49
  318.2 10.5 %copy.66 = f32[512,8,4,128]{3,1,2,0:T(8,128)} copy(f32[512,8,4,128]{0,3,2,1:T(8,128)} %bitcast.104) | data formatting | bytes 16777216 | tf_op jit(solution)/shard_map/reshape | solution.py:61
  328.7 5.6 %bitcast_convert_fusion = bf16[16,512,128]{2,0,1:T(8,128)(2,1)S(1)} fusion(f32[512,8,4,128]{3,1,2,0:T(8,128)} %copy.66, s32[8,4]{0,1:T(4,128)S(1)} %copy-done.8), kind=kOutput, calls=%fused_computation | convolution fusion | flops 403702272 | bytes 10485888 | tf_op jit(solution)/shard_map/rjkc,jkd->rdc/dot_general | solution.py:62
  334.3 1.9 copy.106
  336.2 51.3 %reduce-scatter.11.cloned.1.call-done = bf16[16,1024]{1,0:T(8,128)(2,1)} async-done(((bf16[512,1024]{1,0:T(8,128)(2,1)}), bf16[16,1024]{1,0:T(8,128)(2,1)}) %reduce-scatter.11.cloned.1.call-update) | async-done | bytes 32784 | tf_op jit(solution)/shard_map/reduce_scatter | solution.py:106
  387.5 1.4 convert_element_type.122
  388.9 87.2 %reduce-scatter.9.cloned.1.call-done = bf16[16,1024]{1,0:T(8,128)(2,1)} async-done(((bf16[512,1024]{1,0:T(8,128)(2,1)}), bf16[16,1024]{1,0:T(8,128)(2,1)}) %reduce-scatter.9.cloned.1.call-update) | async-done | bytes 32784 | tf_op jit(solution)/shard_map/reduce_scatter | solution.py:109
  476.1 1.4 convert_element_type.118
  477.4 43.8 %reduce-scatter.7.cloned.1.call-done = bf16[64,2048]{1,0:T(8,128)(2,1)} async-done(((bf16[512,2048]{1,0:T(8,128)(2,1)}), bf16[64,2048]{1,0:T(8,128)(2,1)}) %reduce-scatter.7.cloned.1.call-update) | async-done | bytes 262160 | tf_op jit(solution)/shard_map/reduce_scatter | solution.py:113
  521.2 1.1 fusion.33
  522.4 2.0 fusion.32
  (51 shorter events, 0.5 us)
Async XLA Ops:
  7.2 40.8 %copy-start = (bf16[64,2048]{1,0:T(8,128)(2,1)S(1)}, bf16[64,2048]{1,0:T(8,128)(2,1)}, u32[]{:S(2)}) copy-start(bf16[64,2048]{1,0:T(8,128)(2,1)} %param.9) | copy-start | bytes 786436
  7.2 40.8 %copy-start.7 = (f32[2048]{0:T(1024)S(1)}, f32[2048]{0:T(1024)}, u32[]{:S(2)}) copy-start(f32[2048]{0:T(1024)} %param.10) | copy-start | bytes 24580
  7.2 53.6 %all-gather.4.cloned.1.call-start = ((), (), s32[]{:S(2)}) async-start(), calls=%async_computation.4 | async-start | bytes 1081344 | tf_op jit(solution)/shard_map/all_gather | solution.py:34
  7.9 102.4 %all-gather.6.cloned.1.call-start = ((), (), s32[]{:S(2)}) async-start(), calls=%async_computation.5 | async-start | bytes 1081344 | tf_op jit(solution)/shard_map/all_gather | solution.py:35
  10.2 12.2 %collective-permute-start = (bf16[64,2048]{1,0:T(8,128)(2,1)S(1)}, bf16[64,2048]{1,0:T(8,128)(2,1)S(1)}, u32[]{:S(2)}, u32[]{:S(2)}) collective-permute-start(bf16[64,2048]{1,0:T(8,128)(2,1)S(1)} %fusion.27), channel_id=1, source_target_pairs={{0,1},{1,2},{2,3},{3,4},{4,5},{5,6},{6,7},{7,0},{8,9},{9,10},{10,1... | collective-permute-start | bytes 786440 | tf_op jit(solution)/shard_map/ppermute | solution.py:45
  22.4 8.7 %collective-permute-start.1 = (bf16[64,2048]{1,0:T(8,128)(2,1)S(1)}, bf16[64,2048]{1,0:T(8,128)(2,1)S(1)}, u32[]{:S(2)}, u32[]{:S(2)}) collective-permute-start(bf16[64,2048]{1,0:T(8,128)(2,1)S(1)} %collective-permute-done), channel_id=1, source_target_pairs={{0,1},{1,2},{2,3},{3,4},{4,5},{5,6},{6,7},{7,0},{8,9},{9,10},{10,1... | collective-permute-start | bytes 786440 | tf_op jit(solution)/shard_map/ppermute | solution.py:45
  22.4 8.7 %collective-permute-start.4 = (bf16[64,2048]{1,0:T(8,128)(2,1)S(1)}, bf16[64,2048]{1,0:T(8,128)(2,1)S(1)}, u32[]{:S(2)}, u32[]{:S(2)}) collective-permute-start(bf16[64,2048]{1,0:T(8,128)(2,1)S(1)} %fusion.27), channel_id=1, source_target_pairs={{0,7},{1,0},{2,1},{3,2},{4,3},{5,4},{6,5},{7,6},{8,15},{9,8},{10,9... | collective-permute-start | bytes 786440 | tf_op jit(solution)/shard_map/ppermute | solution.py:47
  31.1 7.8 %collective-permute-start.2 = (bf16[64,2048]{1,0:T(8,128)(2,1)S(1)}, bf16[64,2048]{1,0:T(8,128)(2,1)S(1)}, u32[]{:S(2)}, u32[]{:S(2)}) collective-permute-start(bf16[64,2048]{1,0:T(8,128)(2,1)S(1)} %collective-permute-done.1), channel_id=1, source_target_pairs={{0,1},{1,2},{2,3},{3,4},{4,5},{5,6},{6,7},{7,0},{8,9},{9,10},{10,1... | collective-permute-start | bytes 786440 | tf_op jit(solution)/shard_map/ppermute | solution.py:45
  31.1 7.9 %collective-permute-start.5 = (bf16[64,2048]{1,0:T(8,128)(2,1)S(1)}, bf16[64,2048]{1,0:T(8,128)(2,1)S(1)}, u32[]{:S(2)}, u32[]{:S(2)}) collective-permute-start(bf16[64,2048]{1,0:T(8,128)(2,1)S(1)} %collective-permute-done.4), channel_id=1, source_target_pairs={{0,7},{1,0},{2,1},{3,2},{4,3},{5,4},{6,5},{7,6},{8,15},{9,8},{10,9... | collective-permute-start | bytes 786440 | tf_op jit(solution)/shard_map/ppermute | solution.py:47
  38.9 7.6 %collective-permute-start.3 = (bf16[64,2048]{1,0:T(8,128)(2,1)S(1)}, bf16[64,2048]{1,0:T(8,128)(2,1)S(1)}, u32[]{:S(2)}, u32[]{:S(2)}) collective-permute-start(bf16[64,2048]{1,0:T(8,128)(2,1)S(1)} %collective-permute-done.2), channel_id=1, source_target_pairs={{0,1},{1,2},{2,3},{3,4},{4,5},{5,6},{6,7},{7,0},{8,9},{9,10},{10,1... | collective-permute-start | bytes 786440 | tf_op jit(solution)/shard_map/ppermute | solution.py:45
  39.0 139.7 %reduce-scatter.5.cloned.1.call-start = ((), (), s32[]{:S(2)}) async-start(), calls=%async_computation.6 | async-start | bytes 2359296 | tf_op jit(solution)/shard_map/reduce_scatter | solution.py:71
  39.0 8.7 %collective-permute-start.6 = (bf16[64,2048]{1,0:T(8,128)(2,1)S(1)}, bf16[64,2048]{1,0:T(8,128)(2,1)S(1)}, u32[]{:S(2)}, u32[]{:S(2)}) collective-permute-start(bf16[64,2048]{1,0:T(8,128)(2,1)S(1)} %collective-permute-done.5), channel_id=1, source_target_pairs={{0,7},{1,0},{2,1},{3,2},{4,3},{5,4},{6,5},{7,6},{8,15},{9,8},{10,9... | collective-permute-start | bytes 786440 | tf_op jit(solution)/shard_map/ppermute | solution.py:47
  48.2 0.9 copy-start.8
  134.0 2.0 copy-start.11
  134.0 46.3 %copy-start.9 = (f32[2048]{0:T(1024)S(1)}, f32[2048]{0:T(1024)}, u32[]{:S(2)}) copy-start(f32[2048]{0:T(1024)} %param.17) | copy-start | bytes 24580
  134.0 121.4 %copy-start.10 = (f32[1024]{0:T(1024)S(1)}, f32[1024]{0:T(1024)}, u32[]{:S(2)}) copy-start(f32[1024]{0:T(1024)} %param.15) | copy-start | bytes 12292
  134.0 121.6 %copy-start.4 = (bf16[64,2048]{1,0:T(8,128)(2,1)S(1)}, bf16[64,2048]{1,0:T(8,128)(2,1)}, u32[]{:S(2)}) copy-start(bf16[64,2048]{1,0:T(8,128)(2,1)} %param.16) | copy-start | bytes 786436
  136.0 158.2 %all-gather.8.cloned.1.call-start = ((), (), s32[]{:S(2)}) async-start(), calls=%async_computation.7 | async-start | bytes 2359296 | tf_op jit(solution)/shard_map/all_gather | solution.py:88
  179.7 0.7 copy-start.6
  256.5 131.0 %reduce-scatter.11.cloned.1.call-start = ((), (), s32[]{:S(2)}) async-start(), calls=%async_computation.10 | async-start | bytes 1081344 | tf_op jit(solution)/shard_map/reduce_scatter | solution.py:106
  297.6 1.6 copy-start.3
  298.4 3.9 copy-start.2
  303.6 172.4 %reduce-scatter.9.cloned.1.call-start = ((), (), s32[]{:S(2)}) async-start(), calls=%async_computation.9 | async-start | bytes 1081344 | tf_op jit(solution)/shard_map/reduce_scatter | solution.py:109
  303.7 5.6 %copy-start.1 = (bf16[512,8,4,128]{3,1,2,0:T(8,128)(2,1)S(1)}, bf16[512,8,4,128]{3,1,2,0:T(8,128)(2,1)}, u32[]{:S(2)}) copy-start(bf16[512,8,4,128]{3,1,2,0:T(8,128)(2,1)} %copy.105) | copy-start | bytes 12582916
  313.4 207.8 %reduce-scatter.7.cloned.1.call-start = ((), (), s32[]{:S(2)}) async-start(), calls=%async_computation.8 | async-start | bytes 2359296 | tf_op jit(solution)/shard_map/reduce_scatter | solution.py:113
  334.3 188.0 %copy-start.5 = (bf16[64,2048]{1,0:T(8,128)(2,1)S(1)}, bf16[64,2048]{1,0:T(8,128)(2,1)}, u32[]{:S(2)}) copy-start(bf16[64,2048]{1,0:T(8,128)(2,1)} %param.16) | copy-start | bytes 786436
Sparse Core Ops, SparseCore 0:
  10.6 50.1 all-gather.3
  63.3 46.9 all-gather.5
  136.1 42.5 reduce-scatter.4
  256.6 37.5 all-gather.7
  303.7 83.7 reduce-scatter.10
  391.1 84.8 reduce-scatter.8
  478.6 42.5 reduce-scatter.6
